TPU v7x, 32 devices: a whole 2x2x4 slice. The times are simulated.
32 devices in a mesh: dp: 4 (over y, core), head: 8 (over z, x).
Axes of the slice: x: 2, y: 2, z: 4, core: 2. Of those that a mesh axis runs over, the one named last changes fastest.
Arguments:
- hidden: bfloat16 [12288, 4096], P('dp'), may hold values from -6 to 6
- weight: bfloat16 [2048, 4096], P('head'), may hold values from -0.09375 to 0.09375
- block_ids: int32 [48, 8], P('dp'), may hold values from 0 to 15, all different within a row
- targets: int32 [12288, 8], P('dp'), may hold values from 0 to 2047
Outputs:
- grad_hidden: bfloat16 [12288, 4096], P('dp', 'head')
- grad_weight: bfloat16 [2048, 4096], P('head', 'dp')
Inputs may be any that keep to these rules, and one draw needn't show every extreme that they name: `block_ids`: each row block lists 8 different label blocks; every label block is listed by some row block. `targets`: a row may repeat a label id.
All inputs are finite; a program needn't handle non-finite values.
Results may differ from a plain program's by a relative error of at most 0.014.
Values may be sent and summed in bfloat16 or wider, within the bound.
No kernel may reach another device: no remote copies, remote signals or barrier semaphores. Data moves between devices by JAX's collectives and lax.ppermute only.
A program may use at most 192 MiB of HBM per device.

v0:
```python
import jax
import jax.numpy as jnp
from jax import lax
from jax.sharding import PartitionSpec as P

BLOCK = 128


def local(hidden, weight, block_ids, targets):
    head_count = lax.axis_size("head")
    device = lax.axis_index("head")
    owned = weight.shape[0]
    per_device = owned // BLOCK
    row_blocks = block_ids.shape[0]
    block_rows = hidden.shape[0] // row_blocks
    first = device * per_device
    owned_ids = first + jnp.arange(per_device, dtype=jnp.int32)
    logits = jnp.einsum("rd,ld->rl", hidden, weight, preferred_element_type=jnp.float32)
    slot_match = block_ids[:, :, None] == owned_ids[None, None, :]
    listed = jnp.any(slot_match, axis=1)
    row_mask = jnp.broadcast_to(
        listed[:, None, :, None], (row_blocks, block_rows, per_device, BLOCK)
    )
    row_mask = row_mask.reshape(row_blocks * block_rows, owned)
    labels = first * BLOCK + jnp.arange(owned, dtype=jnp.int32)
    hits = jnp.any(targets[:, :, None] == labels[None, None, :], axis=1)
    signal = jax.nn.sigmoid(logits) - hits.astype(jnp.float32)
    grads = jnp.where(row_mask, signal, 0.0).astype(jnp.bfloat16)
    weight_part = jnp.einsum("rl,rd->ld", grads, hidden, preferred_element_type=jnp.float32)
    grad_weight = lax.psum_scatter(
        weight_part.astype(jnp.bfloat16), "dp", scatter_dimension=1, tiled=True
    )
    grads4 = grads.reshape(row_blocks, block_rows, per_device, BLOCK)
    picker = slot_match.astype(jnp.bfloat16)
    slot_local = jnp.einsum(
        "ikb,irbj->ikrj", picker, grads4, preferred_element_type=jnp.float32
    ).astype(jnp.bfloat16)
    slot_total = lax.psum(slot_local, "head").astype(jnp.float32).astype(jnp.bfloat16)
    columns = lax.all_to_all(weight, "head", split_axis=1, concat_axis=0, tiled=True)
    narrow = columns.shape[1]
    blocks3 = columns.reshape(per_device * head_count, BLOCK, narrow)
    chosen = blocks3[block_ids]
    terms = jnp.einsum("ikrj,ikjd->ikrd", slot_total, chosen, preferred_element_type=jnp.float32)
    groups = jnp.arange(head_count, dtype=jnp.int32)
    owner = ((block_ids // per_device)[:, :, None] == groups[None, None, :]).astype(jnp.float32)
    parts = jnp.einsum("iko,ikrd->iord", owner, terms, precision=lax.Precision.HIGHEST)
    rounded = lax.optimization_barrier(parts.astype(jnp.bfloat16))
    summed = jnp.sum(rounded.astype(jnp.float32), axis=1)
    grad_hidden = summed.reshape(row_blocks * block_rows, narrow).astype(jnp.bfloat16)
    return (grad_hidden, grad_weight)


def solution(mesh):
    return jax.shard_map(
        local,
        mesh=mesh,
        in_specs=(P("dp", None), P("head", None), P("dp", None), P("dp", None)),
        out_specs=(P("dp", "head"), P("head", "dp")),
        check_vma=False,
    )
```

profile of v0, /device:TPU:0, one launch (start us, length us, event | category | flops | bytes accessed | tf_op | source)
XLA Modules:
  0.0 421.9 jit_solution(15903401731539270005)
XLA Ops:
  8.0 0.0 all-reduce.2.cloned.1.call-start
  8.1 0.8 copy.35
  8.8 0.4 compare_reduce_fusion.1
  9.2 0.1 copy.36
  9.3 0.3 broadcast_in_dim.7
  9.7 0.5 copy.46
  10.2 1.8 copy.38
  12.0 1.4 copy.37
  13.3 17.2 %compare_reduce_fusion = pred[3072,256]{1,0:T(8,128)(4,1)S(1)} fusion(s32[256]{0:T(256)S(1)} %iota_add_fusion, s32[3072,8]{1,0:T(8,128)S(1)} %copy.37), kind=kLoop, calls=%fused_computation.3 | loop fusion | flops 11796480 | bytes 885760 | tf_op jit(solution)/shard_map/reduce_or | solution.py:26
  30.5 13.2 %fusion.12 = bf16[3072,256]{1,0:T(8,128)(2,1)S(1)} fusion(pred[3072,256]{1,0:T(32,128)(4,1)} %copy.38, bf16[3072,4096]{1,0:T(8,128)(2,1)} %param.4, bf16[256,4096]{1,0:T(8,128)(2,1)} %param.5, pred[3072,256]{1,0:T(8,128)(4,1)S(1)} %compare_reduce_fusion), kind=kOutput, calls=%fused_computation.14 | convolution fusion | flops 6447955968 | bytes 30408704 | tf_op jit(solution)/shard_map/rd,ld->rl/dot_general | solution.py:18
  43.7 0.0 copy-start.1
  43.7 0.4 reshape.32
  44.2 4.5 %convolution_convert_fusion.1 = bf16[12,8,256,128]{3,1,2,0:T(8,128)(2,1)} fusion(bf16[12,256,2,128]{3,2,1,0:T(2,128)(2,1)S(1)} %reshape.32, s32[12,8]{1,0:T(8,128)S(1)} %copy.35, s32[2]{0:T(128)S(1)} %iota_add_fusion.1), kind=kOutput, calls=%fused_computation.15 | convolution fusion | flops 15728832 | bytes 7864712 | tf_op jit(solution)/shard_map/ikb,irbj->ikrj/dot_general | solution.py:35
  48.7 0.0 all-reduce.2.cloned.1.call-update
  48.7 0.0 copy-done.1
  48.7 4.1 copy.39
  52.8 7.3 %all-to-all-start = ((bf16[256,8,512]{0,2,1:T(8,128)(2,1)}), bf16[256,8,512]{0,2,1:T(8,128)(2,1)S(1)}, u32[]{:S(2)}, u32[]{:S(2)}) async-start(bf16[256,8,512]{0,2,1:T(8,128)(2,1)} %bitcast.29), calls=%async_computation | async-start | bytes 4194304 | tf_op jit(solution)/shard_map/all_to_all | solution.py:39
  60.1 0.0 copy-start.2
  60.1 0.2 reduce-scatter.2.cloned.1.call-start
  60.3 13.1 %convolution_convert_fusion = bf16[256,4096]{1,0:T(8,128)(2,1)} fusion(bf16[3072,256]{1,0:T(8,128)(2,1)} %copy-done.1, bf16[3072,4096]{1,0:T(8,128)(2,1)} %param.4), kind=kOutput, calls=%fused_computation.7 | convolution fusion | flops 6443499520 | bytes 28835840 | tf_op jit(solution)/shard_map/rl,rd->ld/dot_general | solution.py:29
  73.5 0.0 reduce-scatter.2.cloned.1.call-update
  73.5 0.0 copy-done.2
  73.5 0.1 copy.34
  73.6 0.1 copy.41
  73.7 0.1 reshape.36
  73.8 84.4 %all-to-all-done = bf16[256,8,512]{0,2,1:T(8,128)(2,1)S(1)} async-done(((bf16[256,8,512]{0,2,1:T(8,128)(2,1)}), bf16[256,8,512]{0,2,1:T(8,128)(2,1)S(1)}, u32[]{:S(2)}, u32[]{:S(2)}) %all-to-all-start) | async-done | bytes 2097184 | tf_op jit(solution)/shard_map/all_to_all | solution.py:39
  158.1 0.0 copy-start
  158.1 1.3 copy-done
  159.5 2.9 copy.40
  162.3 6.7 %gather_fusion = bf16[96,128,512]{2,1,0:T(8,128)(2,1)} fusion(bf16[16,128,512]{2,1,0:T(8,128)(2,1)S(1)} %bitcast.26, s32[1024]{0:T(1024)S(1)} %pad_clamp_fusion), kind=kCustom, calls=%fused_computation | custom fusion | bytes 25166208 | tf_op jit(solution)/shard_map/gather | solution.py:42
  169.1 137.8 %all-reduce.2.cloned.1.call-done = bf16[12,8,256,128]{3,1,2,0:T(8,128)(2,1)} async-done(((bf16[12,8,256,128]{3,1,2,0:T(8,128)(2,1)}), bf16[12,8,256,128]{3,1,2,0:T(8,128)(2,1)}) %all-reduce.2.cloned.1.call-update) | async-done | bytes 6291472 | tf_op jit(solution)/shard_map/psum | solution.py:38
  306.9 24.0 %fusion.5 = f32[12,8,256,512]{3,2,1,0:T(8,128)} fusion(bf16[12,8,128,512]{3,2,1,0:T(8,128)(2,1)} %bitcast.27, bf16[12,8,256,128]{3,1,2,0:T(8,128)(2,1)} %all-reduce.2.cloned.1.call-done), kind=kOutput, calls=%fused_computation.5 | convolution fusion | flops 3221225472 | bytes 69206016 | tf_op jit(solution)/shard_map/ikrj,ikjd->ikrd/dot_general | solution.py:43
  330.9 61.9 %fusion.2 = bf16[12,8,256,512]{3,1,2,0:T(8,128)(2,1)} fusion(f32[12,8,256,512]{3,2,1,0:T(8,128)} %fusion.5, s32[12,8]{1,0:T(8,128)S(1)} %copy.34), kind=kOutput, calls=%fused_computation.4 | convolution fusion | flops 1220543232 | bytes 75497856 | tf_op jit(solution)/shard_map/iko,ikrd->iord/dot_general | solution.py:46
  392.8 21.7 %reduce_sum.12 = bf16[12,256,512]{2,1,0:T(8,128)(2,1)} reduce(bf16[12,8,256,512]{3,1,2,0:T(8,128)(2,1)} %fusion.2, bf16[]{:T(256)} %constant.32.clone.1), dimensions={1}, to_apply=%region_3.4 | reduce | flops 11010048 | bytes 28311554 | tf_op jit(solution)/shard_map/reduce_sum | solution.py:48
  414.5 0.0 reduce-scatter.2.cloned.1.call-done
  (4 shorter events, 0.0 us)
Async XLA Ops:
  8.0 298.9 %all-reduce.2.cloned.1.call-start = ((), (), s32[]{:S(2)}) async-start(), calls=%async_computation.2 | async-start | bytes 12582912 | tf_op jit(solution)/shard_map/psum | solution.py:38
  43.7 5.0 %copy-start.1 = (bf16[3072,256]{1,0:T(8,128)(2,1)}, bf16[3072,256]{1,0:T(8,128)(2,1)S(1)}, u32[]{:S(2)}) copy-start(bf16[3072,256]{1,0:T(8,128)(2,1)S(1)} %fusion.12) | copy-start | bytes 4718596
  52.8 105.3 %all-to-all-start = ((bf16[256,8,512]{0,2,1:T(8,128)(2,1)}), bf16[256,8,512]{0,2,1:T(8,128)(2,1)S(1)}, u32[]{:S(2)}, u32[]{:S(2)}) async-start(bf16[256,8,512]{0,2,1:T(8,128)(2,1)} %bitcast.29), calls=%async_computation | async-start | bytes 4194304 | tf_op jit(solution)/shard_map/all_to_all | solution.py:39
  60.1 13.4 %copy-start.2 = (s32[12,8]{0,1:T(8,128)S(1)}, s32[12,8]{0,1:T(8,128)}, u32[]{:S(2)}) copy-start(s32[12,8]{0,1:T(8,128)} %param.6) | copy-start | bytes 1156
  60.1 354.4 %reduce-scatter.2.cloned.1.call-start = ((), (), s32[]{:S(2)}) async-start(), calls=%async_computation.3 | async-start | bytes 2621440 | tf_op jit(solution)/shard_map/reduce_scatter | solution.py:30
  158.1 1.3 copy-start
Sparse Core Ops, SparseCore 0:
  48.9 257.9 all-reduce.1
Sparse Core Ops, SparseCore 1:
  73.6 32.3 reduce-scatter.1
where the time goes:
time: 423 us; the launch traced here: 422 us
  waiting for transfers between devices  222 us (52%)
  matrix products  117 us (28%)
  other arithmetic  39.2 us (9%)
  local copies, waits for them, and re-layouts  20.6 us (5%)
  between operations  15.6 us (4%)
  starting transfers between devices  7.54 us (2%)
    psum x1, waiting for transfers between devices, local(): lax.psum(slot_local, 'head').astype(jnp.float32).astype(jnp.bfloat16)  138 us
    all_to_all x1, waiting for transfers between devices, local(): lax.all_to_all(weight, 'head', split_axis=1, concat_axis=0, tiled=True)  84.4 us
    dot_general x1, matrix products, local(): jnp.einsum('iko,ikrd->iord', owner, terms, precision=lax.Precision.HIGHEST)  61.9 us
    dot_general x1, matrix products, local(): jnp.einsum('ikrj,ikjd->ikrd', slot_total, chosen, preferred_element_type=...  24 us
    reduce_sum x1, other arithmetic, local(): summed = jnp.sum(rounded.astype(jnp.float32), axis=1)  21.7 us
    reduce_or x1, other arithmetic, local(): hits = jnp.any(targets[:, :, None] == labels[None, None, :], axis=1)  17.2 us
    dot_general x1, matrix products, local(): jnp.einsum('rd,ld->rl', hidden, weight, preferred_element_type=jnp.float32)  13.2 us
    dot_general x1, matrix products, local(): jnp.einsum('rl,rd->ld', grads, hidden, preferred_element_type=jnp.float32)  13.1 us
  transfers between devices with their start and end apart: 3, of which 2 were waited for; matrix products, arithmetic and copies ran while one was open for 32% of the time, Pallas kernels for 0%

commit v1 on v0

--- a/solution.py
+++ b/solution.py
@@ -4,6 +4,11 @@
 from jax.sharding import PartitionSpec as P
 
 BLOCK = 128
+
+
+def summed_here(x, axis):
+    terms = lax.all_gather(x, axis)
+    return jnp.sum(terms, axis=0)
 
 
 def local(hidden, weight, block_ids, targets):
@@ -35,7 +40,7 @@
     slot_local = jnp.einsum(
         "ikb,irbj->ikrj", picker, grads4, preferred_element_type=jnp.float32
     ).astype(jnp.bfloat16)
-    slot_total = lax.psum(slot_local, "head").astype(jnp.float32).astype(jnp.bfloat16)
+    slot_total = summed_here(slot_local, "head").astype(jnp.float32).astype(jnp.bfloat16)
     columns = lax.all_to_all(weight, "head", split_axis=1, concat_axis=0, tiled=True)
     narrow = columns.shape[1]
     blocks3 = columns.reshape(per_device * head_count, BLOCK, narrow)

time: 423 us -> 1160 us (2.74)
  waiting for transfers between devices: 222 us -> 941 us
  other arithmetic: 39.2 us -> 59.2 us
    all_gather x0 -> x1, waiting for transfers between devices: none -> 884 us  [summed_here(): terms = lax.all_gather(x, axis)]
    psum x1 -> x0, waiting for transfers between devices: 138 us -> none  [local(): lax.psum(slot_local, 'head').astype(jnp.float32).astype(jnp.bfloat16)]
    all_to_all x1, waiting for transfers between devices: 84.4 us -> 56.3 us  [local(): lax.all_to_all(weight, 'head', split_axis=1, concat_axis=0, tiled=True)]
    reduce_sum x0 -> x1, other arithmetic: none -> 20 us  [summed_here(): return jnp.sum(terms, axis=0)]
  transfers between devices with their start and end apart: 3 -> 3, of which waited for: 2 -> 2; matrix products, arithmetic and copies ran while one was open for 32% -> 13% of each run, Pallas kernels for 0% -> 0%
where the time goes in v1:
time: 1160 us
  waiting for transfers between devices  941 us (81%)
  matrix products  116 us (10%)
  other arithmetic  59.2 us (5%)
  local copies, waits for them, and re-layouts  24.9 us (2%)
  between operations  15.6 us (1%)
    all_gather x1, waiting for transfers between devices, summed_here(): terms = lax.all_gather(x, axis)  884 us
    dot_general x1, matrix products, local(): jnp.einsum('iko,ikrd->iord', owner, terms, precision=lax.Precision.HIGHEST)  61.9 us
    all_to_all x1, waiting for transfers between devices, local(): lax.all_to_all(weight, 'head', split_axis=1, concat_axis=0, tiled=True)  56.3 us
    dot_general x1, matrix products, local(): jnp.einsum('ikrj,ikjd->ikrd', slot_total, chosen, preferred_element_type=...  24 us
  transfers between devices with their start and end apart: 3, of which 2 were waited for; matrix products, arithmetic and copies ran while one was open for 13% of the time, Pallas kernels for 0%

profile of v1, /device:TPU:0, one launch (start us, length us, event | category | flops | bytes accessed | tf_op | source)
XLA Modules:
  0.0 1164.0 jit_solution(8509796233300316719)
XLA Ops:
  8.0 0.0 all-gather.3.cloned.1.call-start
  8.1 0.8 copy.36
  8.8 0.4 compare_reduce_fusion.1
  9.2 0.1 copy.37
  9.3 0.3 broadcast_in_dim.7
  9.7 0.5 copy.50
  10.2 1.8 copy.39
  12.0 1.4 copy.38
  13.3 17.2 %compare_reduce_fusion = pred[3072,256]{1,0:T(8,128)(4,1)S(1)} fusion(s32[256]{0:T(256)S(1)} %iota_add_fusion, s32[3072,8]{1,0:T(8,128)S(1)} %copy.38), kind=kLoop, calls=%fused_computation.3 | loop fusion | flops 11796480 | bytes 885760 | tf_op jit(solution)/shard_map/reduce_or | solution.py:31
  30.5 13.2 %fusion.10 = bf16[3072,256]{1,0:T(8,128)(2,1)S(1)} fusion(pred[3072,256]{1,0:T(32,128)(4,1)} %copy.39, bf16[3072,4096]{1,0:T(8,128)(2,1)} %param.4, bf16[256,4096]{1,0:T(8,128)(2,1)} %param.5, pred[3072,256]{1,0:T(8,128)(4,1)S(1)} %compare_reduce_fusion), kind=kOutput, calls=%fused_computation.12 | convolution fusion | flops 6447955968 | bytes 30408704 | tf_op jit(solution)/shard_map/rd,ld->rl/dot_general | solution.py:23
  43.7 0.0 copy-start.1
  43.7 0.4 reshape.32
  44.2 2.8 convolution_convert_fusion.1
  47.0 4.4 copy.40
  51.4 0.0 copy-done.1
  51.4 0.0 copy-start.2
  51.4 0.0 all-gather.3.cloned.1.call-update
  51.4 1.6 copy-done.2
  53.0 2.4 copy.42
  55.4 7.3 all-to-all-start
  62.7 0.0 copy-start.3
  62.7 0.2 reduce-scatter.2.cloned.1.call-start
  62.9 14.3 %convolution_convert_fusion = bf16[256,4096]{1,0:T(8,128)(2,1)} fusion(bf16[3072,256]{1,0:T(8,128)(2,1)} %copy-done.1, bf16[3072,4096]{1,0:T(8,128)(2,1)} %param.4), kind=kOutput, calls=%fused_computation.5 | convolution fusion | flops 6443499520 | bytes 28835840 | tf_op jit(solution)/shard_map/rl,rd->ld/dot_general | solution.py:34
  77.2 0.0 reduce-scatter.2.cloned.1.call-update
  77.2 0.0 copy-done.3
  77.2 0.1 copy.35
  77.3 0.1 copy.44
  77.4 0.1 reshape.36
  77.5 56.3 %all-to-all-done = bf16[256,8,512]{0,2,1:T(8,128)(2,1)S(1)} async-done(((bf16[256,8,512]{0,2,1:T(8,128)(2,1)}), bf16[256,8,512]{0,2,1:T(8,128)(2,1)S(1)}, u32[]{:S(2)}, u32[]{:S(2)}) %all-to-all-start) | async-done | bytes 2097184 | tf_op jit(solution)/shard_map/all_to_all | solution.py:44
  133.8 0.0 copy-start
  133.8 1.3 copy-done
  135.1 2.9 copy.43
  138.0 6.7 gather_fusion
  144.7 884.3 %all-gather.3.cloned.1.call-done = bf16[96,8,256,128]{3,2,1,0:T(8,128)(2,1)} async-done(((bf16[12,8,256,128]{3,2,1,0:T(8,128)(2,1)}), bf16[96,8,256,128]{3,2,1,0:T(8,128)(2,1)}) %all-gather.3.cloned.1.call-update) | async-done | bytes 50331664 | tf_op jit(solution)/shard_map/all_gather | solution.py:10
  1029.0 20.0 %reduce_sum.24 = bf16[12,8,256,128]{3,2,1,0:T(8,128)(2,1)} reduce(bf16[8,12,8,256,128]{4,3,2,1,0:T(8,128)(2,1)} %bitcast.29, bf16[]{:T(256)} %constant.32.clone.1), dimensions={0}, to_apply=%region_2.3 | reduce | flops 22020096 | bytes 56623104 | tf_op jit(solution)/shard_map/reduce_sum | solution.py:11
  1049.0 24.0 %fusion.18 = f32[12,8,256,512]{3,2,1,0:T(8,128)} fusion(bf16[12,8,256,128]{3,2,1,0:T(8,128)(2,1)} %reduce_sum.24, bf16[12,8,128,512]{3,2,1,0:T(8,128)(2,1)} %bitcast.30), kind=kOutput, calls=%fused_computation.32 | convolution fusion | flops 3221225472 | bytes 69206016 | tf_op jit(solution)/shard_map/ikrj,ikjd->ikrd/dot_general | solution.py:48
  1073.0 61.9 %fusion.2 = bf16[12,8,256,512]{3,1,2,0:T(8,128)(2,1)} fusion(f32[12,8,256,512]{3,2,1,0:T(8,128)} %fusion.18, s32[12,8]{1,0:T(8,128)S(1)} %copy.35), kind=kOutput, calls=%fused_computation.4 | convolution fusion | flops 1220543232 | bytes 75497856 | tf_op jit(solution)/shard_map/iko,ikrd->iord/dot_general | solution.py:51
  1134.9 21.7 %reduce_sum.25 = bf16[12,256,512]{2,1,0:T(8,128)(2,1)} reduce(bf16[12,8,256,512]{3,1,2,0:T(8,128)(2,1)} %fusion.2, bf16[]{:T(256)} %constant.32.clone.1), dimensions={1}, to_apply=%region_3.4 | reduce | flops 11010048 | bytes 28311554 | tf_op jit(solution)/shard_map/reduce_sum | solution.py:53
  1156.6 0.0 reduce-scatter.2.cloned.1.call-done
  (4 shorter events, 0.0 us)
Async XLA Ops:
  8.0 1021.0 %all-gather.3.cloned.1.call-start = ((), (), s32[]{:S(2)}) async-start(), calls=%async_computation.3 | async-start | bytes 56623104 | tf_op jit(solution)/shard_map/all_gather | solution.py:10
  43.7 7.6 copy-start.1
  51.4 1.6 copy-start.2
  55.4 78.4 %all-to-all-start = ((bf16[256,8,512]{0,2,1:T(8,128)(2,1)}), bf16[256,8,512]{0,2,1:T(8,128)(2,1)S(1)}, u32[]{:S(2)}, u32[]{:S(2)}) async-start(bf16[256,8,512]{0,2,1:T(8,128)(2,1)} %bitcast.32), calls=%async_computation | async-start | bytes 4194304 | tf_op jit(solution)/shard_map/all_to_all | solution.py:44
  62.7 14.5 %copy-start.3 = (s32[12,8]{0,1:T(8,128)S(1)}, s32[12,8]{0,1:T(8,128)}, u32[]{:S(2)}) copy-start(s32[12,8]{0,1:T(8,128)} %param.6) | copy-start | bytes 1156
  62.7 1093.9 %reduce-scatter.2.cloned.1.call-start = ((), (), s32[]{:S(2)}) async-start(), calls=%async_computation.2 | async-start | bytes 2621440 | tf_op jit(solution)/shard_map/reduce_scatter | solution.py:35
  133.8 1.3 copy-start
Sparse Core Ops, SparseCore 0:
  51.5 977.4 all-gather.2
Sparse Core Ops, SparseCore 1:
  77.3 32.4 reduce-scatter.1
